TPU v7x, 32 devices: a whole 2x2x4 slice. The times are simulated.
32 devices in a mesh: tok: 8 (over z, y), voc: 4 (over x, core).
Axes of the slice: x: 2, y: 2, z: 4, core: 2. Of those that a mesh axis runs over, the one named last changes fastest.
Arguments:
- teacher_logits: bfloat16 [1024, 76032], P('tok', 'voc'), may hold values from -1000 to 1000
- student_logits: bfloat16 [1024, 76032], P('tok', 'voc'), may hold values from -1000 to 1000
- target_ids: int32 [1024], P('tok'), may hold values from -1 to 76031, as said below
- vocab_used: int32 [76032], replicated, may hold values from 0 to 1
Outputs:
- logit_grad: bfloat16 [1024, 76032], P('tok', 'voc')
- token_loss: float32 [1024], P('tok')
Inputs may be any that keep to these rules, and one draw needn't show every extreme that they name: `target_ids`: every entry that is not -1 names a vocabulary entry v with vocab_used[v] == 1; the first token of every 128 is never -1.
All inputs are finite; a program needn't handle non-finite values.
Results may differ from a plain program's by a relative error of at most 0.0004.
Values may be sent and summed in bfloat16 or wider, within the bound.
No kernel may reach another device: no remote copies, remote signals or barrier semaphores. Data moves between devices by JAX's collectives and lax.ppermute only.
A program may use at most 64 MiB of HBM per device.

v0:
```python
import jax
import jax.numpy as jnp
from jax import lax
from jax.sharding import PartitionSpec as P

SENTINEL = -1e30


def combined_all(value, axis, join):
    pieces = jax.tree.map(lambda part: lax.all_gather(part, axis), value)
    head = jax.tree.map(lambda part: part[0], pieces)
    tail = jax.tree.map(lambda part: part[1:], pieces)
    subtotal, _ = lax.scan(lambda subtotal, slab: (join(subtotal, slab), None), head, tail)
    return subtotal


def local_totals(values, used):
    top_value = jnp.max(jnp.where(used, values, SENTINEL), axis=1)
    total = jnp.sum(jnp.where(used, jnp.exp(values - top_value[:, None]), 0.0), axis=1)
    return (top_value, total)


def merge_pair(first, second):
    top_value = jnp.maximum(first[0], second[0])
    total = first[1] * jnp.exp(first[0] - top_value) + second[1] * jnp.exp(second[0] - top_value)
    return (top_value, total)


def merge_joint(first, second):
    teacher_top = jnp.maximum(first[0], second[0])
    scale_one = jnp.exp(first[0] - teacher_top)
    scale_two = jnp.exp(second[0] - teacher_top)
    student_top, student_sum = merge_pair((first[3], first[4]), (second[3], second[4]))
    return (
        teacher_top,
        first[1] * scale_one + second[1] * scale_two,
        first[2] * scale_one + second[2] * scale_two,
        student_top,
        student_sum,
        first[5] + second[5],
    )


def body(teacher_logits, student_logits, target_ids, vocab_used):
    tok_rows, vocab_cols = teacher_logits.shape
    voc_count = lax.axis_size("voc")
    voc_index = lax.axis_index("voc")
    block_cols = vocab_cols // voc_count
    total_tokens = tok_rows * lax.axis_size("tok")
    kept = target_ids >= 0
    kept_count = lax.psum(jnp.sum(kept.astype(jnp.float32)), "tok")
    hard_weight = jnp.where(kept, 0.5 * total_tokens / kept_count, 0.0)
    position = jnp.arange(vocab_cols, dtype=jnp.int32)
    student_cols = (
        position // block_cols * voc_count + voc_index
    ) * block_cols + position % block_cols
    teacher_here = lax.all_to_all(
        teacher_logits.reshape(tok_rows, voc_count, block_cols),
        "voc",
        split_axis=1,
        concat_axis=1,
        tiled=True,
    ).reshape(tok_rows, vocab_cols)
    used = (vocab_used[student_cols] == 1)[None, :]
    onehot = student_cols[None, :] == target_ids[:, None]
    teacher = teacher_here.astype(jnp.float32)
    student = student_logits.astype(jnp.float32)
    student_top, student_sum = local_totals(student, used)
    target_part = jnp.sum(jnp.where(onehot, student, 0.0), axis=1)
    teacher_top, teacher_sum = local_totals(teacher, used)
    weighted = jnp.sum(
        jnp.where(used, jnp.exp(teacher - teacher_top[:, None]) * (teacher - student), 0.0), axis=1
    )
    teacher_top, teacher_sum, weighted, student_top, student_sum, target_logit = combined_all(
        (teacher_top, teacher_sum, weighted, student_top, student_sum, target_part),
        "voc",
        merge_joint,
    )
    teacher_lse = teacher_top + jnp.log(teacher_sum)
    student_lse = student_top + jnp.log(student_sum)
    teacher_prob = jnp.where(used, jnp.exp(teacher - teacher_lse[:, None]), 0.0)
    divergence = weighted / teacher_sum - teacher_lse + student_lse
    student_prob = jnp.where(used, jnp.exp(student - student_lse[:, None]), 0.0)
    gradient = 0.5 * (student_prob - teacher_prob) + hard_weight[:, None] * (
        student_prob - onehot.astype(jnp.float32)
    )
    gradient = jnp.where(used, gradient, 0.0).astype(jnp.bfloat16)
    token_loss = 0.5 * divergence + hard_weight * (student_lse - target_logit)
    return (gradient, token_loss)


def solution(mesh):
    placed = (P("tok", "voc"), P("tok", "voc"), P("tok"), P())
    return jax.shard_map(
        body, mesh=mesh, in_specs=placed, out_specs=(P("tok", "voc"), P("tok")), check_vma=False
    )
```

profile of v0, /device:TPU:0, one launch (start us, length us, event | category | flops | bytes accessed | tf_op | source)
XLA Modules:
  0.0 223.0 jit_solution(9439695803364014107)
XLA Ops:
  0.6 0.0 copy-start
  0.6 0.0 copy-start.1
  0.7 5.1 %all-to-all-start = ((bf16[128,4,4752]{0,2,1:T(8,128)(2,1)}), bf16[128,4,4752]{0,2,1:T(8,128)(2,1)}, u32[]{:S(2)}, u32[]{:S(2)}) async-start(bf16[128,4,4752]{0,2,1:T(8,128)(2,1)} %bitcast.95), calls=%async_computation | async-start | bytes 9732096 | tf_op jit(solution)/shard_map/all_to_all | solution.py:57
  5.8 0.0 copy-done.1
  5.8 0.6 fusion.55
  6.4 23.8 %psum.7 = f32[]{:T(128)} all-reduce(f32[]{:T(128)} %fusion.55), channel_id=1, replica_groups=mesh['tok'=8,'voc'=4] {'tok'}, use_global_device_ids=true, to_apply=%region_9.10 | all-reduce | flops 1 | bytes 8 | tf_op jit(solution)/shard_map/psum | solution.py:51
  30.1 0.6 fusion.51
  30.7 0.0 copy-done
  30.8 97.7 %gather_fusion = s32[19008]{0:T(1024)S(1)} fusion(s32[76032]{0:T(1024)S(1)} %copy-done, s32[19456]{0:T(1024)S(1)} %pad_clamp_fusion), kind=kCustom, calls=%fused_computation | custom fusion | bytes 228096 | tf_op jit(solution)/shard_map/gather | solution.py:64
  128.5 0.1 eq.28
  128.7 13.7 %fusion.27 = (f32[128]{0:T(128)S(1)}, f32[128]{0:T(128)S(1)}) fusion(bf16[128,19008]{0,1:T(8,128)(2,1)} %param.7, s32[128]{0:T(128)S(1)} %copy-done.1, s32[19008]{0:T(1024)S(1)} %fusion.48, pred[19008]{0:T(1024)(128)(4,1)S(1)} %broadcast_compare_fusion), kind=kLoop, calls=%fused_computation.42 | loop fusion | flops 14597888 | bytes 4962624 | tf_op jit(solution)/shard_map/reduce_sum | solution.py:69
  142.4 5.1 %all-gather.11 = f32[4,1,128]{2,1,0:T(1,128)S(1)} all-gather(f32[1,1,128]{2,1,0:T(1,128)S(1)} %bitcast.106), channel_id=7, replica_groups=mesh['tok'=8,'voc'=4] {'voc'}, dimensions={0}, use_global_device_ids=true | all-gather | bytes 2560 | tf_op jit(solution)/shard_map/all_gather | solution.py:10
  147.5 5.3 %all-gather.9 = f32[4,1,128]{2,1,0:T(1,128)S(1)} all-gather(f32[1,1,128]{2,1,0:T(1,128)S(1)} %bitcast.103), channel_id=5, replica_groups=mesh['tok'=8,'voc'=4] {'voc'}, dimensions={0}, use_global_device_ids=true | all-gather | bytes 2560 | tf_op jit(solution)/shard_map/all_gather | solution.py:10
  153.5 0.0 all-to-all-done
  153.5 10.4 %fusion.32 = f32[128]{0:T(128)S(1)} fusion(bf16[128,4,4752]{0,2,1:T(8,128)(2,1)} %all-to-all-done, pred[4,4752]{1,0:T(4,128)(4,1)S(1)} %eq.28), kind=kLoop, calls=%fused_computation.51 | loop fusion | flops 7298944 | bytes 4885568 | tf_op jit(solution)/shard_map/reduce_max | solution.py:18
  163.9 12.6 %fusion.26 = (f32[128]{0:T(128)S(1)}, f32[128]{0:T(128)S(1)}) fusion(bf16[128,19008]{0,1:T(8,128)(2,1)} %param.7, f32[128]{0:T(128)S(1)} %get-tuple-element.83, pred[19008]{0:T(1024)(128)(4,1)S(1)} %broadcast_compare_fusion, f32[128]{0:T(128)S(1)} %fusion.32, bf16[128,4,4752]{0,2,1:T(8,128)(2,1)} %all-to-all-done), kind=kLoop, calls=%fused_computation.41 | loop fusion | flops 24329984 | bytes 9753152 | tf_op jit(solution)/shard_map/reduce_sum | solution.py:19
  176.6 5.1 %all-gather.8 = f32[4,1,128]{2,1,0:T(1,128)S(1)} all-gather(f32[1,1,128]{2,1,0:T(1,128)S(1)} %bitcast.105), channel_id=4, replica_groups=mesh['tok'=8,'voc'=4] {'voc'}, dimensions={0}, use_global_device_ids=true | all-gather | bytes 2560 | tf_op jit(solution)/shard_map/all_gather | solution.py:10
  181.6 5.0 %all-gather.10 = f32[4,1,128]{2,1,0:T(1,128)S(1)} all-gather(f32[1,1,128]{2,1,0:T(1,128)S(1)} %bitcast.104), channel_id=6, replica_groups=mesh['tok'=8,'voc'=4] {'voc'}, dimensions={0}, use_global_device_ids=true | all-gather | bytes 2560 | tf_op jit(solution)/shard_map/all_gather | solution.py:10
  186.7 10.4 %fusion.35 = f32[128]{0:T(128)S(1)} fusion(bf16[128,4,4752]{0,2,1:T(8,128)(2,1)} %all-to-all-done, f32[128]{0:T(128)S(1)} %fusion.32, pred[4,4752]{1,0:T(4,128)(4,1)S(1)} %eq.28), kind=kLoop, calls=%fused_computation.54 | loop fusion | flops 9731968 | bytes 4886080 | tf_op jit(solution)/shard_map/reduce_sum | solution.py:19
  197.0 5.1 %all-gather.7 = f32[4,1,128]{2,1,0:T(1,128)S(1)} all-gather(f32[1,1,128]{2,1,0:T(1,128)S(1)} %bitcast.107), channel_id=3, replica_groups=mesh['tok'=8,'voc'=4] {'voc'}, dimensions={0}, use_global_device_ids=true | all-gather | bytes 2560 | tf_op jit(solution)/shard_map/all_gather | solution.py:10
  202.1 5.0 %all-gather.6 = f32[4,1,128]{2,1,0:T(1,128)S(1)} all-gather(f32[1,1,128]{2,1,0:T(1,128)S(1)} %bitcast.102), channel_id=2, replica_groups=mesh['tok'=8,'voc'=4] {'voc'}, dimensions={0}, use_global_device_ids=true | all-gather | bytes 2560 | tf_op jit(solution)/shard_map/all_gather | solution.py:10
  207.2 0.3 while.20
  207.5 0.5 multiply_add_fusion
  208.0 15.0 %fusion.19 = bf16[128,19008]{0,1:T(8,128)(2,1)} fusion(bf16[128,19008]{0,1:T(8,128)(2,1)} %param.7, bf16[128,4,4752]{0,2,1:T(8,128)(2,1)} %all-to-all-done, f32[128]{0:T(128)S(1)} %get-tuple-element.116, f32[128]{0:T(128)S(1)} %get-tuple-element.118, f32[128]{0:T(128)S(1)} %get-tuple-element.115, s32[128]{0:T(128)S(1)} %copy-done.1, s32[19008]{0:T(1024)S(1)} %fusion.48, ...), kind=kLoop, calls=%fused_computation.34 | loop fusion | flops 36495360 | bytes 14695232 | tf_op jit(solution)/shard_map/convert_element_type | solution.py:87
  (33 shorter events, 0.3 us)
Async XLA Ops:
  0.6 30.1 %copy-start = (s32[76032]{0:T(1024)S(1)}, s32[76032]{0:T(1024)}, u32[]{:S(2)}) copy-start(s32[76032]{0:T(1024)} %param.9) | copy-start | bytes 912388
  0.6 5.1 %copy-start.1 = (s32[128]{0:T(128)S(1)}, s32[128]{0:T(128)}, u32[]{:S(2)}) copy-start(s32[128]{0:T(128)} %param.8) | copy-start | bytes 1540
  0.7 152.9 %all-to-all-start = ((bf16[128,4,4752]{0,2,1:T(8,128)(2,1)}), bf16[128,4,4752]{0,2,1:T(8,128)(2,1)}, u32[]{:S(2)}, u32[]{:S(2)}) async-start(bf16[128,4,4752]{0,2,1:T(8,128)(2,1)} %bitcast.95), calls=%async_computation | async-start | bytes 9732096 | tf_op jit(solution)/shard_map/all_to_all | solution.py:57
where the time goes:
time: 224 us; the launch traced here: 223 us
  local copies, waits for them, and re-layouts  97.9 us (44%)
  other arithmetic  64.1 us (29%)
  blocking collectives  54.4 us (24%)
  starting transfers between devices  5.11 us (2%)
    gather x1, local copies, waits for them, and re-layouts, body(): used = (vocab_used[student_cols] == 1)[None, :]  97.7 us
    all_gather x6, blocking collectives, combined_all(): pieces = jax.tree.map(lambda part: lax.all_gather(part, axis), value)  30.6 us
    psum x1, blocking collectives, body(): kept_count = lax.psum(jnp.sum(kept.astype(jnp.float32)), 'tok')  23.8 us
    reduce_sum x2, other arithmetic, local_totals(): jnp.sum(jnp.where(used, jnp.exp(values - top_value[:, None]), 0.0), axis=1)  23 us
    convert_element_type x1, other arithmetic, body(): gradient = jnp.where(used, gradient, 0.0).astype(jnp.bfloat16)  15 us
    reduce_sum x1, other arithmetic, body(): target_part = jnp.sum(jnp.where(onehot, student, 0.0), axis=1)  13.7 us
    reduce_max x1, other arithmetic, local_totals(): top_value = jnp.max(jnp.where(used, values, SENTINEL), axis=1)  10.4 us
    all_to_all x1, starting transfers between devices, body(): lax.all_to_all(teacher_logits.reshape(tok_rows, voc_count, block_cols), '...  5.11 us
  transfers between devices with their start and end apart: 1, of which 0 were waited for; matrix products, arithmetic and copies ran while one was open for 51% of the time, Pallas kernels for 0%

commit v1 on v0

--- a/solution.py
+++ b/solution.py
@@ -2,6 +2,7 @@
 import jax.numpy as jnp
 from jax import lax
 from jax.sharding import PartitionSpec as P
+from jax.lax import all_to_all, axis_size
 
 SENTINEL = -1e30
 
@@ -54,12 +55,20 @@
     student_cols = (
         position // block_cols * voc_count + voc_index
     ) * block_cols + position % block_cols
-    teacher_here = lax.all_to_all(
-        teacher_logits.reshape(tok_rows, voc_count, block_cols),
-        "voc",
-        split_axis=1,
-        concat_axis=1,
-        tiled=True,
+    teacher_here = jnp.concatenate(
+        all_to_all(
+            jnp.stack(
+                jnp.split(
+                    teacher_logits.reshape(tok_rows, voc_count, block_cols),
+                    axis_size("voc"),
+                    axis=1,
+                )
+            ),
+            "voc",
+            split_axis=0,
+            concat_axis=0,
+        ),
+        axis=1,
     ).reshape(tok_rows, vocab_cols)
     used = (vocab_used[student_cols] == 1)[None, :]
     onehot = student_cols[None, :] == target_ids[:, None]

time: 224 us -> 230 us (1.027)
  local copies, waits for them, and re-layouts: 97.9 us -> 101 us
  other arithmetic: 64.1 us -> 67 us
    another operation x0 -> x1, other arithmetic: none -> 2.74 us  [body(): jnp.stack(jnp.split(teacher_logits.reshape(tok_rows, voc_count, block_col...]
    another operation x0 -> x1, local copies, waits for them, and re-layouts: none -> 2.74 us  [body(): jnp.stack(jnp.split(teacher_logits.reshape(tok_rows, voc_count, block_col...]
  transfers between devices with their start and end apart: 1 -> 1, of which waited for: 0 -> 0; matrix products, arithmetic and copies ran while one was open for 51% -> 49% of each run, Pallas kernels for 0% -> 0%
where the time goes in v1:
time: 230 us; the launch traced here: 229 us
  local copies, waits for them, and re-layouts  101 us (44%)
  other arithmetic  67 us (29%)
  blocking collectives  54.4 us (24%)
  starting transfers between devices  5.1 us (2%)
    gather x1, local copies, waits for them, and re-layouts, body(): used = (vocab_used[student_cols] == 1)[None, :]  97.7 us
    all_gather x6, blocking collectives, combined_all(): pieces = jax.tree.map(lambda part: lax.all_gather(part, axis), value)  30.6 us
    psum x1, blocking collectives, body(): kept_count = lax.psum(jnp.sum(kept.astype(jnp.float32)), 'tok')  23.8 us
    reduce_sum x2, other arithmetic, local_totals(): jnp.sum(jnp.where(used, jnp.exp(values - top_value[:, None]), 0.0), axis=1)  23 us
    convert_element_type x1, other arithmetic, body(): gradient = jnp.where(used, gradient, 0.0).astype(jnp.bfloat16)  15.1 us
    reduce_sum x1, other arithmetic, body(): target_part = jnp.sum(jnp.where(onehot, student, 0.0), axis=1)  13.7 us
    reduce_max x1, other arithmetic, local_totals(): top_value = jnp.max(jnp.where(used, values, SENTINEL), axis=1)  10.4 us
    all_to_all x1, starting transfers between devices, body(): all_to_all(jnp.stack(jnp.split(teacher_logits.reshape(tok_rows, voc_count...  5.1 us
  transfers between devices with their start and end apart: 1, of which 0 were waited for; matrix products, arithmetic and copies ran while one was open for 49% of the time, Pallas kernels for 0%

profile of v1, /device:TPU:0, one launch (start us, length us, event | category | flops | bytes accessed | tf_op | source)
XLA Modules:
  0.0 228.7 jit_solution(3239623152381461153)
XLA Ops:
  0.6 0.0 copy-start
  0.6 2.7 %slice_bitcast_fusion.3 = (bf16[1,128,1,4752]{1,3,2,0:T(8,128)(2,1)S(1)}, bf16[1,128,1,4752]{1,3,2,0:T(8,128)(2,1)S(1)}, bf16[1,128,1,4752]{1,3,2,0:T(8,128)(2,1)S(1)}, bf16[1,128,1,4752]{1,3,2,0:T(8,128)(2,1)S(1)}) fusion(bf16[128,4,4752]{0,2,1:T(8,128)(2,1)} %bitcast.105), kind=kLoop, calls=%fused_computation.62 | loop fusion | bytes 9732096 | tf_op jit(solution)/shard_map/stack | solution.py:60
  3.4 2.7 %pad_maximum_fusion = bf16[4,128,1,4752]{1,3,2,0:T(8,128)(2,1)} fusion(bf16[1,128,1,4752]{1,3,2,0:T(8,128)(2,1)S(1)} %get-tuple-element.119, bf16[1,128,1,4752]{1,3,2,0:T(8,128)(2,1)S(1)} %get-tuple-element.120, bf16[1,128,1,4752]{1,3,2,0:T(8,128)(2,1)S(1)} %get-tuple-element.121, bf16[1,128,1,4752]{1,3,2,0:T(8,128)(2,1)S(1)} %get-tuple-element.118), kind=kLoop, calls=%fused_computation.58 | loop fusion | flops 7299072 | bytes 9732096 | tf_op jit(solution)/shard_map/stack | solution.py:60
  6.1 0.0 copy-start.1
  6.1 5.1 %all-to-all-start = ((bf16[4,128,1,4752]{1,3,2,0:T(8,128)(2,1)}), bf16[4,128,1,4752]{1,3,2,0:T(8,128)(2,1)}, u32[]{:S(2)}, u32[]{:S(2)}) async-start(bf16[4,128,1,4752]{1,3,2,0:T(8,128)(2,1)} %pad_maximum_fusion), calls=%async_computation | async-start | bytes 9732096 | tf_op jit(solution)/shard_map/all_to_all | solution.py:59
  11.2 0.0 copy-done.1
  11.3 0.6 fusion.55
  11.9 23.8 %psum.7 = f32[]{:T(128)} all-reduce(f32[]{:T(128)} %fusion.55), channel_id=1, replica_groups=mesh['tok'=8,'voc'=4] {'tok'}, use_global_device_ids=true, to_apply=%region_9.10 | all-reduce | flops 1 | bytes 8 | tf_op jit(solution)/shard_map/psum | solution.py:52
  35.7 0.6 fusion.51
  36.3 0.0 copy-done
  36.3 97.7 %gather_fusion = s32[19008]{0:T(1024)S(1)} fusion(s32[76032]{0:T(1024)S(1)} %copy-done, s32[19456]{0:T(1024)S(1)} %pad_clamp_fusion), kind=kCustom, calls=%fused_computation | custom fusion | bytes 228096 | tf_op jit(solution)/shard_map/gather | solution.py:73
  134.1 0.1 eq.28
  134.2 13.7 %fusion.27 = (f32[128]{0:T(128)S(1)}, f32[128]{0:T(128)S(1)}) fusion(bf16[128,19008]{0,1:T(8,128)(2,1)} %param.7, s32[128]{0:T(128)S(1)} %copy-done.1, s32[19008]{0:T(1024)S(1)} %fusion.48, pred[19008]{0:T(1024)(128)(4,1)S(1)} %broadcast_compare_fusion), kind=kLoop, calls=%fused_computation.42 | loop fusion | flops 14597888 | bytes 4962624 | tf_op jit(solution)/shard_map/reduce_sum | solution.py:78
  148.0 5.1 %all-gather.9 = f32[4,1,128]{2,1,0:T(1,128)S(1)} all-gather(f32[1,1,128]{2,1,0:T(1,128)S(1)} %bitcast.113), channel_id=5, replica_groups=mesh['tok'=8,'voc'=4] {'voc'}, dimensions={0}, use_global_device_ids=true | all-gather | bytes 2560 | tf_op jit(solution)/shard_map/all_gather | solution.py:11
  153.0 5.3 %all-gather.11 = f32[4,1,128]{2,1,0:T(1,128)S(1)} all-gather(f32[1,1,128]{2,1,0:T(1,128)S(1)} %bitcast.115), channel_id=7, replica_groups=mesh['tok'=8,'voc'=4] {'voc'}, dimensions={0}, use_global_device_ids=true | all-gather | bytes 2560 | tf_op jit(solution)/shard_map/all_gather | solution.py:11
  159.1 0.0 all-to-all-done
  159.1 10.4 %fusion.32 = f32[128]{0:T(128)S(1)} fusion(bf16[4,128,1,4752]{1,3,2,0:T(8,128)(2,1)} %all-to-all-done, pred[4,4752]{1,0:T(4,128)(4,1)S(1)} %eq.28), kind=kLoop, calls=%fused_computation.51 | loop fusion | flops 7298944 | bytes 4885568 | tf_op jit(solution)/shard_map/reduce_max | solution.py:19
  169.5 12.6 %fusion.26 = (f32[128]{0:T(128)S(1)}, f32[128]{0:T(128)S(1)}) fusion(bf16[128,19008]{0,1:T(8,128)(2,1)} %param.7, f32[128]{0:T(128)S(1)} %get-tuple-element.83, pred[19008]{0:T(1024)(128)(4,1)S(1)} %broadcast_compare_fusion, f32[128]{0:T(128)S(1)} %fusion.32, bf16[4,128,1,4752]{1,3,2,0:T(8,128)(2,1)} %all-to-all-done), kind=kLoop, calls=%fused_computation.41 | loop fusion | flops 24329984 | bytes 9753152 | tf_op jit(solution)/shard_map/reduce_sum | solution.py:20
  182.1 5.1 %all-gather.10 = f32[4,1,128]{2,1,0:T(1,128)S(1)} all-gather(f32[1,1,128]{2,1,0:T(1,128)S(1)} %bitcast.116), channel_id=6, replica_groups=mesh['tok'=8,'voc'=4] {'voc'}, dimensions={0}, use_global_device_ids=true | all-gather | bytes 2560 | tf_op jit(solution)/shard_map/all_gather | solution.py:11
  187.2 5.0 %all-gather.8 = f32[4,1,128]{2,1,0:T(1,128)S(1)} all-gather(f32[1,1,128]{2,1,0:T(1,128)S(1)} %bitcast.114), channel_id=4, replica_groups=mesh['tok'=8,'voc'=4] {'voc'}, dimensions={0}, use_global_device_ids=true | all-gather | bytes 2560 | tf_op jit(solution)/shard_map/all_gather | solution.py:11
  192.3 10.4 %fusion.35 = f32[128]{0:T(128)S(1)} fusion(bf16[4,128,1,4752]{1,3,2,0:T(8,128)(2,1)} %all-to-all-done, f32[128]{0:T(128)S(1)} %fusion.32, pred[4,4752]{1,0:T(4,128)(4,1)S(1)} %eq.28), kind=kLoop, calls=%fused_computation.54 | loop fusion | flops 9731968 | bytes 4886080 | tf_op jit(solution)/shard_map/reduce_sum | solution.py:20
  202.6 5.1 %all-gather.7 = f32[4,1,128]{2,1,0:T(1,128)S(1)} all-gather(f32[1,1,128]{2,1,0:T(1,128)S(1)} %bitcast.117), channel_id=3, replica_groups=mesh['tok'=8,'voc'=4] {'voc'}, dimensions={0}, use_global_device_ids=true | all-gather | bytes 2560 | tf_op jit(solution)/shard_map/all_gather | solution.py:11
  207.7 5.0 %all-gather.6 = f32[4,1,128]{2,1,0:T(1,128)S(1)} all-gather(f32[1,1,128]{2,1,0:T(1,128)S(1)} %bitcast.112), channel_id=2, replica_groups=mesh['tok'=8,'voc'=4] {'voc'}, dimensions={0}, use_global_device_ids=true | all-gather | bytes 2560 | tf_op jit(solution)/shard_map/all_gather | solution.py:11
  212.8 0.3 while.20
  213.1 0.5 multiply_add_fusion
  213.6 15.1 %fusion.19 = bf16[128,19008]{0,1:T(8,128)(2,1)} fusion(bf16[128,19008]{0,1:T(8,128)(2,1)} %param.7, bf16[4,128,1,4752]{1,3,2,0:T(8,128)(2,1)} %all-to-all-done, f32[128]{0:T(128)S(1)} %get-tuple-element.116, f32[128]{0:T(128)S(1)} %get-tuple-element.122, f32[128]{0:T(128)S(1)} %get-tuple-element.115, s32[128]{0:T(128)S(1)} %copy-done.1, ...), kind=kLoop, calls=%fused_computation.34 | loop fusion | flops 36495360 | bytes 14695232 | tf_op jit(solution)/shard_map/convert_element_type | solution.py:96
  (33 shorter events, 0.3 us)
Async XLA Ops:
  0.6 35.7 %copy-start = (s32[76032]{0:T(1024)S(1)}, s32[76032]{0:T(1024)}, u32[]{:S(2)}) copy-start(s32[76032]{0:T(1024)} %param.9) | copy-start | bytes 912388
  6.1 5.1 %copy-start.1 = (s32[128]{0:T(128)S(1)}, s32[128]{0:T(128)}, u32[]{:S(2)}) copy-start(s32[128]{0:T(128)} %param.8) | copy-start | bytes 1540
  6.1 153.0 %all-to-all-start = ((bf16[4,128,1,4752]{1,3,2,0:T(8,128)(2,1)}), bf16[4,128,1,4752]{1,3,2,0:T(8,128)(2,1)}, u32[]{:S(2)}, u32[]{:S(2)}) async-start(bf16[4,128,1,4752]{1,3,2,0:T(8,128)(2,1)} %pad_maximum_fusion), calls=%async_computation | async-start | bytes 9732096 | tf_op jit(solution)/shard_map/all_to_all | solution.py:59
